TPU v7x, 32 devices: a whole 2x2x4 slice. The times are simulated.
32 devices in a mesh: groups: 2 (over y), ep: 4 (over z), sub: 2 (over x), tp: 2 (over core).
Axes of the slice: x: 2, y: 2, z: 4, core: 2. Of those that a mesh axis runs over, the one named last changes fastest.
Arguments:
- rows: bfloat16 [1024, 4096], P(('groups', 'ep'), ('sub', 'tp')), parts along dimension 0, may hold values from -6 to 6
- path: int32 [4, 1024, 1], P(None, ('groups', 'ep')), parts along dimension 1, may hold values from 0 to 7; in each aligned block of 128 rows (0 to 127, 128 to 255, ..., all dimensions but the last counted through in order) at most 32 rows name the same one
- norm_gain: float32 [8, 4096], P(('ep', 'tp')), may hold values from 0.1 to 1.9
- gate_weight: bfloat16 [8, 1408, 4096], P(('ep', 'tp'), 'sub'), may hold values from -0.09375 to 0.09375
- up_weight: bfloat16 [8, 1408, 4096], P(('ep', 'tp'), 'sub'), may hold values from -0.09375 to 0.09375
- down_weight: bfloat16 [8, 1408, 4096], P(('ep', 'tp'), 'sub'), may hold values from -0.15625 to 0.15625
Outputs:
- chained: bfloat16 [1024, 4096], P(('groups', 'ep'), ('sub', 'tp')), parts along dimension 0
There are 2 independent parts, one for each index of `groups`. A program takes and returns all parts, laid end to end along the dimension named above; an argument that names none is the same for every part. Nothing has to cross between parts.
Inputs may be any that keep to these rules, and one draw needn't show every extreme that they name: `path`: in each aligned block of 128 rows of one hop no expert is named by more than 32 rows, and in some blocks one expert is named by exactly 32.
All inputs are finite; a program needn't handle non-finite values.
Results may differ from a plain program's by a relative error of at most 0.02.
Values may be sent and summed in bfloat16 or wider, within the bound.
No kernel may reach another device: no remote copies, remote signals or barrier semaphores. Data moves between devices by JAX's collectives and lax.ppermute only.
A program may use at most 64 MiB of HBM per device.

v0:
```python
import functools

import jax
import jax.numpy as jnp
from jax import lax
from jax.experimental import pallas as pl
from jax.experimental.pallas import tpu as pltpu
from jax.sharding import PartitionSpec as P

EPS = 1e-06
BF16 = jnp.bfloat16
F32 = jnp.float32
VMEM = pl.BlockSpec(memory_space=pltpu.VMEM)
SMEM = pl.BlockSpec(memory_space=pltpu.SMEM)


def call(body, outs, *operands, scalars=0, limit=12 << 20, scratch=(), flops=0):
    specs = [SMEM] * scalars + [VMEM] * (len(operands) - scalars)
    moved = sum(o.size * o.dtype.itemsize for o in operands) + sum(
        o.size * o.dtype.itemsize for o in outs
    )
    return pl.pallas_call(
        body,
        out_shape=outs,
        in_specs=specs,
        out_specs=[VMEM] * len(outs),
        scratch_shapes=list(scratch),
        compiler_params=pltpu.CompilerParams(vmem_limit_bytes=limit),
        cost_estimate=pl.CostEstimate(flops=flops, bytes_accessed=moved, transcendentals=0),
    )(*operands)


def swap(value, axis, step):
    return lax.ppermute(value, axis, [(i, i ^ step) for i in range(lax.axis_size(axis))])


def route_body(tp_count, capacity, relative, place_ref, path_ref, mine_ref, other_ref, pick_ref):
    ep_index, core_index = place_ref[0], place_ref[2]
    hops, local_rows, _ = path_ref.shape
    slots = mine_ref.shape[2]
    lane = lax.broadcasted_iota(jnp.int32, (local_rows, slots), 1)
    row = lax.broadcasted_iota(jnp.int32, (local_rows, local_rows), 0)
    col = lax.broadcasted_iota(jnp.int32, (local_rows, local_rows), 1)
    earlier = (col < row).astype(BF16)
    for hop in range(hops):
        expert = path_ref[hop]
        onehot = (expert == lane).astype(F32)
        before = jnp.dot(earlier, onehot.astype(BF16), preferred_element_type=F32)
        rank = jnp.sum(before * onehot, axis=1, keepdims=True).astype(jnp.int32)
        dest, core = lax.div(expert, tp_count), lax.rem(expert, tp_count)
        if relative:
            dest = lax.bitwise_xor(dest, ep_index)
        target = dest * capacity + rank
        here = jnp.where(core == core_index, target, -1) == lane
        there = jnp.where(core == core_index, -1, target) == lane
        mine_ref[hop] = here.astype(BF16)
        other_ref[hop] = there.astype(BF16)
        pick_ref[hop] = here.astype(F32).T.astype(BF16)


def first_body(width, place_ref, own_ref, far_ref, pick_ref, state_ref, *piece_refs):
    core = place_ref[2]
    state_ref[:, pl.ds(pl.multiple_of(core * width, width), width)] = own_ref[...]
    state_ref[:, pl.ds(pl.multiple_of((1 - core) * width, width), width)] = far_ref[...]
    pack(state_ref[...], pick_ref[...], piece_refs)


def pack(state, pick, piece_refs):
    height = piece_refs[0].shape[0]
    packed = jnp.dot(pick, state, preferred_element_type=F32).astype(BF16)
    for s, ref in enumerate(piece_refs):
        ref[...] = packed[s * height : (s + 1) * height]


def turn_body(block, weight_ref, out_ref):
    for b in range(weight_ref.shape[1] // block):
        out_ref[b * block : (b + 1) * block, :] = weight_ref[:, b * block : (b + 1) * block].T


def expert_body(count, sub_count, place_ref, *refs):
    x = place_ref[1]
    data = refs[: count * sub_count]
    gain_ref, gate_ref, up_ref, down_ref = refs[count * sub_count : count * sub_count + 4]
    out_refs = refs[count * sub_count + 4 :]
    width = data[0].shape[1]
    capacity = data[0].shape[0]
    total = 0.0
    values = []
    for u in range(sub_count):
        part = jnp.concatenate([data[i * sub_count + u][...] for i in range(count)], axis=0)
        part = part.astype(F32)
        values.append(part)
        total = total + jnp.sum(part * part, axis=-1, keepdims=True)
    scale = lax.rsqrt(total / (width * sub_count) + EPS)
    gate = up = 0.0
    for u in range(sub_count):
        columns = pl.ds(pl.multiple_of(lax.bitwise_xor(x, u) * width, width), width)
        normed = (values[u] * scale * gain_ref[:, columns]).astype(BF16)
        gate = gate + jnp.dot(normed, gate_ref[columns, :], preferred_element_type=F32)
        up = up + jnp.dot(normed, up_ref[columns, :], preferred_element_type=F32)
    hidden = (gate / (1.0 + jnp.exp(-gate)) * up).astype(BF16)
    for u in range(sub_count):
        columns = pl.ds(pl.multiple_of(lax.bitwise_xor(x, u) * width, width), width)
        partial = jnp.dot(hidden, down_ref[:, columns], preferred_element_type=F32).astype(BF16)
        for i in range(count):
            out_refs[i * sub_count + u][...] = partial[i * capacity : (i + 1) * capacity]


def sum_body(*refs):
    total = refs[0][...].astype(F32)
    for ref in refs[1:-1]:
        total = total + ref[...].astype(F32)
    refs[-1][...] = total.astype(BF16)


def home_body(count, *refs):
    mine, others = refs[:count], refs[count : 2 * count]
    state_ref, here_ref, there_ref, pick_ref, new_ref = refs[2 * count : 2 * count + 5]
    slots = jnp.concatenate([ref[...] for ref in mine], axis=0)
    far = jnp.concatenate([ref[...] for ref in others], axis=0)
    update = jnp.dot(here_ref[...], slots, preferred_element_type=F32)
    update = update + jnp.dot(there_ref[...], far, preferred_element_type=F32)
    state = (state_ref[...].astype(F32) + update).astype(BF16)
    new_ref[...] = state
    pack(state, pick_ref[...], refs[2 * count + 5 :])


def last_body(count, width, place_ref, *refs):
    core = place_ref[2]
    mine, others = refs[:count], refs[count : 2 * count]
    state_ref, here_ref, there_ref, out_ref = refs[2 * count :]
    columns = pl.ds(pl.multiple_of(core * width, width), width)
    slots = jnp.concatenate([ref[:, columns] for ref in mine], axis=0)
    far = jnp.concatenate([ref[:, columns] for ref in others], axis=0)
    update = jnp.dot(here_ref[...], slots, preferred_element_type=F32)
    update = update + jnp.dot(there_ref[...], far, preferred_element_type=F32)
    out_ref[...] = (state_ref[:, columns].astype(F32) + update).astype(BF16)


def shards(rows, path, norm_gain, gate_weight, up_weight, down_weight):
    local_rows, width = rows.shape
    hops = path.shape[0]
    ep_count, sub_count, tp_count = (lax.axis_size(a) for a in ("ep", "sub", "tp"))
    capacity = 2 * local_rows // (ep_count * tp_count)
    slots = ep_count * capacity
    half = width * tp_count
    features = half * sub_count
    hidden = gate_weight.shape[1]
    place = jnp.stack([lax.axis_index(a) for a in ("ep", "sub", "tp")]).astype(jnp.int32)
    relative = ep_count <= 4 and ep_count & (ep_count - 1) == 0
    count = ep_count if relative else 1
    height = slots // count
    piece = jax.ShapeDtypeStruct((height, half), BF16)
    whole = jax.ShapeDtypeStruct((local_rows, half), BF16)

    def across(value, s):
        if not relative:
            value = value.reshape(ep_count, capacity, half)
            return lax.all_to_all(value, "ep", 0, 0, tiled=True).reshape(slots, half)
        return value if s == 0 else swap(value, "ep", s)

    far = swap(rows, "tp", 1)
    square = (hops, local_rows, slots)
    here, there, pick = call(
        functools.partial(route_body, tp_count, capacity, relative),
        [jax.ShapeDtypeStruct(s, BF16) for s in (square, square, (hops, slots, local_rows))],
        place, path, scalars=1,
    )
    state, *pieces = call(
        functools.partial(first_body, width),
        [whole] + [piece] * count,
        place, rows, far, pick[0], scalars=1,
    )
    groups = ((2, 0), (3, 1)) if count == 4 else (tuple(range(count)),)
    order = [s for pair in zip(*groups) for s in pair]
    for hop in range(hops):
        if hop == 0:
            gate = turn(gate_weight[0])
            up = turn(up_weight[0])
            weights = (gate, up, down_weight[0])
        arrived, full, back = {}, {}, {}
        for s in order:
            arrived[s] = across(pieces[s], s)
        for s in order:
            full[s] = [arrived[s]] + [swap(arrived[s], "sub", u) for u in range(1, sub_count)]
        for members in groups:
            partial = call(
                functools.partial(expert_body, len(members), sub_count),
                [piece] * (len(members) * sub_count),
                place, *[p for s in members for p in full[s]], norm_gain, *weights,
                scalars=1, limit=16 << 20,
                flops=6 * len(members) * height * hidden * features,
            )
            for i, s in enumerate(members):
                parts = partial[i * sub_count : (i + 1) * sub_count]
                parts = [parts[0]] + [swap(parts[u], "sub", u) for u in range(1, sub_count)]
                (back[s],) = call(sum_body, [piece], *parts)
        mine, others = [], []
        for s in range(count):
            mine.append(across(back[s], s))
            others.append(swap(mine[s], "tp", 1))
        if hop + 1 < hops:
            state, *pieces = call(
                functools.partial(home_body, count),
                [whole] + [piece] * count,
                *mine, *others, state, here[hop], there[hop], pick[hop + 1],
            )
        else:
            (state,) = call(
                functools.partial(last_body, count, width),
                [jax.ShapeDtypeStruct(rows.shape, BF16)],
                place, *mine, *others, state, here[hop], there[hop], scalars=1,
            )
    return state


def turn(weight, block=512):
    out = jax.ShapeDtypeStruct(weight.shape[::-1], BF16)
    return call(functools.partial(turn_body, block), [out], weight)[0]


def solution(mesh):
    in_specs = (
        P(("groups", "ep"), ("sub", "tp")),
        P(None, ("groups", "ep"), None),
        P(("ep", "tp"), None),
        P(("ep", "tp"), "sub", None),
        P(("ep", "tp"), "sub", None),
        P(("ep", "tp"), "sub", None),
    )
    out_specs = P(("groups", "ep"), ("sub", "tp"))
    return jax.shard_map(shards, mesh=mesh, in_specs=in_specs, out_specs=out_specs, check_vma=False)
```

profile of v0, /device:TPU:0, one launch (start us, length us, event | category | flops | bytes accessed | tf_op | source)
XLA Modules:
  0.0 194.0 jit_solution(7575756197241989729)
XLA Ops:
  4.6 3.6 %collective-permute-start.1 = (bf16[32,2048]{1,0:T(8,128)(2,1)S(1)}, bf16[32,2048]{1,0:T(8,128)(2,1)S(1)}, u32[]{:S(2)}, u32[]{:S(2)}) collective-permute-start(bf16[32,2048]{1,0:T(8,128)(2,1)S(1)} %get-tuple-element.61), channel_id=1, source_target_pairs={{0,8},{4,12},{8,0},{12,4},{1,9},{5,13},{9,1},{13,5},{2,10},{6,14},... | collective-permute-start | bytes 393224 | tf_op jit(solution)/shard_map/ppermute | solution.py:34
  11.3 6.9 %collective-permute-done.1.refs_0_ = bf16[32,2048]{1,0:T(8,128)(2,1)S(1)} collective-permute-done((bf16[32,2048]{1,0:T(8,128)(2,1)S(1)}, bf16[32,2048]{1,0:T(8,128)(2,1)S(1)}, u32[]{:S(2)}, u32[]{:S(2)}) %collective-permute-start.1) | collective-permute-done | bytes 131104 | tf_op jit(solution)/shard_map/ppermute | solution.py:34
  29.2 4.1 %shard_map.68 = (bf16[32,2048]{1,0:T(8,128)(2,1)S(1)}, bf16[32,2048]{1,0:T(8,128)(2,1)S(1)}, bf16[32,2048]{1,0:T(8,128)(2,1)S(1)}, bf16[32,2048]{1,0:T(8,128)(2,1)S(1)}) custom-call(s32[3]{0:T(128)S(1)} %pad_add_fusion.place_ref, bf16[32,2048]{1,0:T(8,128)(2,1)S(1)} %collective-permute-done.1.refs_0_, bf16[32,2048]{1,0:T(8,128)(2,1)S(1)} %collective-permute-done.2.refs_1_, ...), custom_call_target="tpu_custom_call" | custom-call | flops 1107296256 | bytes 18366476 | tf_op jit(solution)/shard_map/pallas_call | solution.py:22
  33.7 4.2 %shard_map.70 = (bf16[32,2048]{1,0:T(8,128)(2,1)S(1)}, bf16[32,2048]{1,0:T(8,128)(2,1)S(1)}, bf16[32,2048]{1,0:T(8,128)(2,1)S(1)}, bf16[32,2048]{1,0:T(8,128)(2,1)S(1)}) custom-call(s32[3]{0:T(128)S(1)} %pad_add_fusion.place_ref, bf16[32,2048]{1,0:T(8,128)(2,1)S(1)} %collective-permute-done.5.refs_0_, bf16[32,2048]{1,0:T(8,128)(2,1)S(1)} %collective-permute-done.6.refs_1_, ...), custom_call_target="tpu_custom_call" | custom-call | flops 1107296256 | bytes 18366476 | tf_op jit(solution)/shard_map/pallas_call | solution.py:22
  41.8 3.5 %collective-permute-start.12 = (bf16[32,2048]{1,0:T(8,128)(2,1)S(1)}, bf16[32,2048]{1,0:T(8,128)(2,1)S(1)}, u32[]{:S(2)}, u32[]{:S(2)}) collective-permute-start(bf16[32,2048]{1,0:T(8,128)(2,1)S(1)} %shard_map.72), channel_id=1, source_target_pairs={{0,8},{4,12},{8,0},{12,4},{1,9},{5,13},{9,1},{13,5},{2,10},{6,14},... | collective-permute-start | bytes 393224 | tf_op jit(solution)/shard_map/ppermute | solution.py:34
  47.2 3.4 %collective-permute-start.14 = (bf16[32,2048]{1,0:T(8,128)(2,1)S(1)}, bf16[32,2048]{1,0:T(8,128)(2,1)S(1)}, u32[]{:S(2)}, u32[]{:S(2)}) collective-permute-start(bf16[32,2048]{1,0:T(8,128)(2,1)S(1)} %shard_map.73), channel_id=1, source_target_pairs={{0,12},{4,8},{8,4},{12,0},{1,13},{5,9},{9,5},{13,1},{2,14},{6,10},... | collective-permute-start | bytes 393224 | tf_op jit(solution)/shard_map/ppermute | solution.py:34
  61.4 3.8 %collective-permute-done.23.refs_0_ = bf16[32,2048]{1,0:T(8,128)(2,1)S(1)} collective-permute-done((bf16[32,2048]{1,0:T(8,128)(2,1)S(1)}, bf16[32,2048]{1,0:T(8,128)(2,1)S(1)}, u32[]{:S(2)}, u32[]{:S(2)}) %collective-permute-start.23) | collective-permute-done | bytes 131104 | tf_op jit(solution)/shard_map/ppermute | solution.py:34
  74.2 4.3 %shard_map.77 = (bf16[32,2048]{1,0:T(8,128)(2,1)S(1)}, bf16[32,2048]{1,0:T(8,128)(2,1)S(1)}, bf16[32,2048]{1,0:T(8,128)(2,1)S(1)}, bf16[32,2048]{1,0:T(8,128)(2,1)S(1)}) custom-call(s32[3]{0:T(128)S(1)} %pad_add_fusion.place_ref, bf16[32,2048]{1,0:T(8,128)(2,1)S(1)} %collective-permute-done.23.refs_0_, bf16[32,2048]{1,0:T(8,128)(2,1)S(1)} %collective-permute-done.24.refs_1_, ...), custom_call_target="tpu_custom_call" | custom-call | flops 1107296256 | bytes 18366476 | tf_op jit(solution)/shard_map/pallas_call | solution.py:22
  80.6 4.2 %shard_map.75 = (bf16[32,2048]{1,0:T(8,128)(2,1)S(1)}, bf16[32,2048]{1,0:T(8,128)(2,1)S(1)}, bf16[32,2048]{1,0:T(8,128)(2,1)S(1)}, bf16[32,2048]{1,0:T(8,128)(2,1)S(1)}) custom-call(s32[3]{0:T(128)S(1)} %pad_add_fusion.place_ref, bf16[32,2048]{1,0:T(8,128)(2,1)S(1)} %collective-permute-done.19.refs_0_, bf16[32,2048]{1,0:T(8,128)(2,1)S(1)} %collective-permute-done.20.refs_1_, ...), custom_call_target="tpu_custom_call" | custom-call | flops 1107296256 | bytes 18366476 | tf_op jit(solution)/shard_map/pallas_call | solution.py:22
  86.9 3.4 %collective-permute-start.28 = (bf16[32,2048]{1,0:T(8,128)(2,1)S(1)}, bf16[32,2048]{1,0:T(8,128)(2,1)S(1)}, u32[]{:S(2)}, u32[]{:S(2)}) collective-permute-start(bf16[32,2048]{1,0:T(8,128)(2,1)S(1)} %shard_map.78), channel_id=1, source_target_pairs={{0,4},{4,0},{8,12},{12,8},{1,5},{5,1},{9,13},{13,9},{2,6},{6,2},{1... | collective-permute-start | bytes 393224 | tf_op jit(solution)/shard_map/ppermute | solution.py:34
  106.6 3.8 %collective-permute-done.41.refs_0_ = bf16[32,2048]{1,0:T(8,128)(2,1)S(1)} collective-permute-done((bf16[32,2048]{1,0:T(8,128)(2,1)S(1)}, bf16[32,2048]{1,0:T(8,128)(2,1)S(1)}, u32[]{:S(2)}, u32[]{:S(2)}) %collective-permute-start.41) | collective-permute-done | bytes 131104 | tf_op jit(solution)/shard_map/ppermute | solution.py:34
  111.4 3.9 %collective-permute-done.43.refs_2_ = bf16[32,2048]{1,0:T(8,128)(2,1)S(1)} collective-permute-done((bf16[32,2048]{1,0:T(8,128)(2,1)S(1)}, bf16[32,2048]{1,0:T(8,128)(2,1)S(1)}, u32[]{:S(2)}, u32[]{:S(2)}) %collective-permute-start.43) | collective-permute-done | bytes 131104 | tf_op jit(solution)/shard_map/ppermute | solution.py:34
  118.1 3.6 %collective-permute-done.44.refs_3_ = bf16[32,2048]{1,0:T(8,128)(2,1)S(1)} collective-permute-done((bf16[32,2048]{1,0:T(8,128)(2,1)S(1)}, bf16[32,2048]{1,0:T(8,128)(2,1)S(1)}, u32[]{:S(2)}, u32[]{:S(2)}) %collective-permute-start.44) | collective-permute-done | bytes 131104 | tf_op jit(solution)/shard_map/ppermute | solution.py:34
  121.7 4.1 %shard_map.84 = (bf16[32,2048]{1,0:T(8,128)(2,1)S(1)}, bf16[32,2048]{1,0:T(8,128)(2,1)S(1)}, bf16[32,2048]{1,0:T(8,128)(2,1)S(1)}, bf16[32,2048]{1,0:T(8,128)(2,1)S(1)}) custom-call(s32[3]{0:T(128)S(1)} %pad_add_fusion.place_ref, bf16[32,2048]{1,0:T(8,128)(2,1)S(1)} %collective-permute-done.41.refs_0_, bf16[32,2048]{1,0:T(8,128)(2,1)S(1)} %collective-permute-done.42.refs_1_, ...), custom_call_target="tpu_custom_call" | custom-call | flops 1107296256 | bytes 18366476 | tf_op jit(solution)/shard_map/pallas_call | solution.py:22
  127.9 4.2 %shard_map.82 = (bf16[32,2048]{1,0:T(8,128)(2,1)S(1)}, bf16[32,2048]{1,0:T(8,128)(2,1)S(1)}, bf16[32,2048]{1,0:T(8,128)(2,1)S(1)}, bf16[32,2048]{1,0:T(8,128)(2,1)S(1)}) custom-call(s32[3]{0:T(128)S(1)} %pad_add_fusion.place_ref, bf16[32,2048]{1,0:T(8,128)(2,1)S(1)} %collective-permute-done.37.refs_0_, bf16[32,2048]{1,0:T(8,128)(2,1)S(1)} %collective-permute-done.38.refs_1_, ...), custom_call_target="tpu_custom_call" | custom-call | flops 1107296256 | bytes 18366476 | tf_op jit(solution)/shard_map/pallas_call | solution.py:22
  141.5 4.9 %collective-permute-done.48.refs_2_ = bf16[32,2048]{1,0:T(8,128)(2,1)S(1)} collective-permute-done((bf16[32,2048]{1,0:T(8,128)(2,1)S(1)}, bf16[32,2048]{1,0:T(8,128)(2,1)S(1)}, u32[]{:S(2)}, u32[]{:S(2)}) %collective-permute-start.48) | collective-permute-done | bytes 131104 | tf_op jit(solution)/shard_map/ppermute | solution.py:34
  149.7 3.2 %collective-permute-start.55 = (bf16[32,2048]{1,0:T(8,128)(2,1)S(1)}, bf16[32,2048]{1,0:T(8,128)(2,1)S(1)}, u32[]{:S(2)}, u32[]{:S(2)}) collective-permute-start(bf16[32,2048]{1,0:T(8,128)(2,1)S(1)} %get-tuple-element.102), channel_id=1, source_target_pairs={{0,8},{4,12},{8,0},{12,4},{1,9},{5,13},{9,1},{13,5},{2,10},{6,14},... | collective-permute-start | bytes 393224 | tf_op jit(solution)/shard_map/ppermute | solution.py:34
  152.9 3.9 %collective-permute-done.59.refs_0_ = bf16[32,2048]{1,0:T(8,128)(2,1)S(1)} collective-permute-done((bf16[32,2048]{1,0:T(8,128)(2,1)S(1)}, bf16[32,2048]{1,0:T(8,128)(2,1)S(1)}, u32[]{:S(2)}, u32[]{:S(2)}) %collective-permute-start.59) | collective-permute-done | bytes 131104 | tf_op jit(solution)/shard_map/ppermute | solution.py:34
  157.5 3.1 %collective-permute-done.61.refs_2_ = bf16[32,2048]{1,0:T(8,128)(2,1)S(1)} collective-permute-done((bf16[32,2048]{1,0:T(8,128)(2,1)S(1)}, bf16[32,2048]{1,0:T(8,128)(2,1)S(1)}, u32[]{:S(2)}, u32[]{:S(2)}) %collective-permute-start.61) | collective-permute-done | bytes 131104 | tf_op jit(solution)/shard_map/ppermute | solution.py:34
  163.4 3.5 %collective-permute-done.62.refs_3_ = bf16[32,2048]{1,0:T(8,128)(2,1)S(1)} collective-permute-done((bf16[32,2048]{1,0:T(8,128)(2,1)S(1)}, bf16[32,2048]{1,0:T(8,128)(2,1)S(1)}, u32[]{:S(2)}, u32[]{:S(2)}) %collective-permute-start.62) | collective-permute-done | bytes 131104 | tf_op jit(solution)/shard_map/ppermute | solution.py:34
  166.9 4.2 %shard_map.91 = (bf16[32,2048]{1,0:T(8,128)(2,1)S(1)}, bf16[32,2048]{1,0:T(8,128)(2,1)S(1)}, bf16[32,2048]{1,0:T(8,128)(2,1)S(1)}, bf16[32,2048]{1,0:T(8,128)(2,1)S(1)}) custom-call(s32[3]{0:T(128)S(1)} %pad_add_fusion.place_ref, bf16[32,2048]{1,0:T(8,128)(2,1)S(1)} %collective-permute-done.59.refs_0_, bf16[32,2048]{1,0:T(8,128)(2,1)S(1)} %collective-permute-done.60.refs_1_, ...), custom_call_target="tpu_custom_call" | custom-call | flops 1107296256 | bytes 18366476 | tf_op jit(solution)/shard_map/pallas_call | solution.py:22
  173.2 4.2 %shard_map.89 = (bf16[32,2048]{1,0:T(8,128)(2,1)S(1)}, bf16[32,2048]{1,0:T(8,128)(2,1)S(1)}, bf16[32,2048]{1,0:T(8,128)(2,1)S(1)}, bf16[32,2048]{1,0:T(8,128)(2,1)S(1)}) custom-call(s32[3]{0:T(128)S(1)} %pad_add_fusion.place_ref, bf16[32,2048]{1,0:T(8,128)(2,1)S(1)} %collective-permute-done.55.refs_0_, bf16[32,2048]{1,0:T(8,128)(2,1)S(1)} %collective-permute-done.56.refs_1_, ...), custom_call_target="tpu_custom_call" | custom-call | flops 1107296256 | bytes 18366476 | tf_op jit(solution)/shard_map/pallas_call | solution.py:22
  183.9 2.9 %collective-permute-done.64.refs_1_ = bf16[32,2048]{1,0:T(8,128)(2,1)S(1)} collective-permute-done((bf16[32,2048]{1,0:T(8,128)(2,1)S(1)}, bf16[32,2048]{1,0:T(8,128)(2,1)S(1)}, u32[]{:S(2)}, u32[]{:S(2)}) %collective-permute-start.64) | collective-permute-done | bytes 131104 | tf_op jit(solution)/shard_map/ppermute | solution.py:34
  187.4 3.8 %collective-permute-done.66.refs_2_ = bf16[32,2048]{1,0:T(8,128)(2,1)S(1)} collective-permute-done((bf16[32,2048]{1,0:T(8,128)(2,1)S(1)}, bf16[32,2048]{1,0:T(8,128)(2,1)S(1)}, u32[]{:S(2)}, u32[]{:S(2)}) %collective-permute-start.66) | collective-permute-done | bytes 131104 | tf_op jit(solution)/shard_map/ppermute | solution.py:34
  (171 shorter events, 98.7 us)
Async XLA Ops:
  4.6 13.7 %collective-permute-start.1 = (bf16[32,2048]{1,0:T(8,128)(2,1)S(1)}, bf16[32,2048]{1,0:T(8,128)(2,1)S(1)}, u32[]{:S(2)}, u32[]{:S(2)}) collective-permute-start(bf16[32,2048]{1,0:T(8,128)(2,1)S(1)} %get-tuple-element.61), channel_id=1, source_target_pairs={{0,8},{4,12},{8,0},{12,4},{1,9},{5,13},{9,1},{13,5},{2,10},{6,14},... | collective-permute-start | bytes 393224 | tf_op jit(solution)/shard_map/ppermute | solution.py:34
  8.2 11.8 %collective-permute-start.5 = (bf16[32,2048]{1,0:T(8,128)(2,1)S(1)}, bf16[32,2048]{1,0:T(8,128)(2,1)S(1)}, u32[]{:S(2)}, u32[]{:S(2)}) collective-permute-start(bf16[32,2048]{1,0:T(8,128)(2,1)S(1)} %get-tuple-element.65), channel_id=1, source_target_pairs={{0,12},{4,8},{8,4},{12,0},{1,13},{5,9},{9,5},{13,1},{2,14},{6,10},... | collective-permute-start | bytes 393224 | tf_op jit(solution)/shard_map/ppermute | solution.py:34
  9.6 10.7 %collective-permute-start.7 = (bf16[32,2048]{1,0:T(8,128)(2,1)S(1)}, bf16[32,2048]{1,0:T(8,128)(2,1)S(1)}, u32[]{:S(2)}, u32[]{:S(2)}) collective-permute-start(bf16[32,2048]{1,0:T(8,128)(2,1)S(1)} %get-tuple-element.66), channel_id=1, source_target_pairs={{0,4},{4,0},{8,12},{12,8},{1,5},{5,1},{9,13},{13,9},{2,6},{6,2},{1... | collective-permute-start | bytes 393224 | tf_op jit(solution)/shard_map/ppermute | solution.py:34
  9.8 19.3 %collective-permute-start.3 = (bf16[32,2048]{1,0:T(8,128)(2,1)S(1)}, bf16[32,2048]{1,0:T(8,128)(2,1)S(1)}, u32[]{:S(2)}, u32[]{:S(2)}) collective-permute-start(bf16[32,2048]{1,0:T(8,128)(2,1)S(1)} %get-tuple-element.62.refs_2_), channel_id=1, source_target_pairs={{0,2},{2,0},{1,3},{3,1},{4,6},{6,4},{5,7},{7,5},{8,10},{10,8},{9,1... | collective-permute-start | bytes 393224 | tf_op jit(solution)/shard_map/ppermute | solution.py:34
  18.2 10.9 %collective-permute-start.2 = (bf16[32,2048]{1,0:T(8,128)(2,1)S(1)}, bf16[32,2048]{1,0:T(8,128)(2,1)S(1)}, u32[]{:S(2)}, u32[]{:S(2)}) collective-permute-start(bf16[32,2048]{1,0:T(8,128)(2,1)S(1)} %collective-permute-done.1.refs_0_), channel_id=1, source_target_pairs={{0,2},{2,0},{1,3},{3,1},{4,6},{6,4},{5,7},{7,5},{8,10},{10,8},{9,1... | collective-permute-start | bytes 393224 | tf_op jit(solution)/shard_map/ppermute | solution.py:34
  20.0 13.6 %collective-permute-start.6 = (bf16[32,2048]{1,0:T(8,128)(2,1)S(1)}, bf16[32,2048]{1,0:T(8,128)(2,1)S(1)}, u32[]{:S(2)}, u32[]{:S(2)}) collective-permute-start(bf16[32,2048]{1,0:T(8,128)(2,1)S(1)} %collective-permute-done.5.refs_0_), channel_id=1, source_target_pairs={{0,2},{2,0},{1,3},{3,1},{4,6},{6,4},{5,7},{7,5},{8,10},{10,8},{9,1... | collective-permute-start | bytes 393224 | tf_op jit(solution)/shard_map/ppermute | solution.py:34
  20.2 13.4 %collective-permute-start.8 = (bf16[32,2048]{1,0:T(8,128)(2,1)S(1)}, bf16[32,2048]{1,0:T(8,128)(2,1)S(1)}, u32[]{:S(2)}, u32[]{:S(2)}) collective-permute-start(bf16[32,2048]{1,0:T(8,128)(2,1)S(1)} %collective-permute-done.7.refs_2_), channel_id=1, source_target_pairs={{0,2},{2,0},{1,3},{3,1},{4,6},{6,4},{5,7},{7,5},{8,10},{10,8},{9,1... | collective-permute-start | bytes 393224 | tf_op jit(solution)/shard_map/ppermute | solution.py:34
  39.9 10.7 %collective-permute-start.4 = (bf16[32,2048]{1,0:T(8,128)(2,1)S(1)}, bf16[32,2048]{1,0:T(8,128)(2,1)S(1)}, u32[]{:S(2)}, u32[]{:S(2)}) collective-permute-start(bf16[32,2048]{1,0:T(8,128)(2,1)S(1)} %get-tuple-element.64), channel_id=1, source_target_pairs={{0,2},{2,0},{1,3},{3,1},{4,6},{6,4},{5,7},{7,5},{8,10},{10,8},{9,1... | collective-permute-start | bytes 393224 | tf_op jit(solution)/shard_map/ppermute | solution.py:34
  41.8 10.5 %collective-permute-start.12 = (bf16[32,2048]{1,0:T(8,128)(2,1)S(1)}, bf16[32,2048]{1,0:T(8,128)(2,1)S(1)}, u32[]{:S(2)}, u32[]{:S(2)}) collective-permute-start(bf16[32,2048]{1,0:T(8,128)(2,1)S(1)} %shard_map.72), channel_id=1, source_target_pairs={{0,8},{4,12},{8,0},{12,4},{1,9},{5,13},{9,1},{13,5},{2,10},{6,14},... | collective-permute-start | bytes 393224 | tf_op jit(solution)/shard_map/ppermute | solution.py:34
  60.5 11.7 %collective-permute-start.19 = (bf16[32,2048]{1,0:T(8,128)(2,1)S(1)}, bf16[32,2048]{1,0:T(8,128)(2,1)S(1)}, u32[]{:S(2)}, u32[]{:S(2)}) collective-permute-start(bf16[32,2048]{1,0:T(8,128)(2,1)S(1)} %get-tuple-element.76), channel_id=1, source_target_pairs={{0,8},{4,12},{8,0},{12,4},{1,9},{5,13},{9,1},{13,5},{2,10},{6,14},... | collective-permute-start | bytes 393224 | tf_op jit(solution)/shard_map/ppermute | solution.py:34
  69.1 11.5 %collective-permute-start.21 = (bf16[32,2048]{1,0:T(8,128)(2,1)S(1)}, bf16[32,2048]{1,0:T(8,128)(2,1)S(1)}, u32[]{:S(2)}, u32[]{:S(2)}) collective-permute-start(bf16[32,2048]{1,0:T(8,128)(2,1)S(1)} %get-tuple-element.77.refs_2_), channel_id=1, source_target_pairs={{0,2},{2,0},{1,3},{3,1},{4,6},{6,4},{5,7},{7,5},{8,10},{10,8},{9,1... | collective-permute-start | bytes 393224 | tf_op jit(solution)/shard_map/ppermute | solution.py:34
  72.2 8.4 %collective-permute-start.20 = (bf16[32,2048]{1,0:T(8,128)(2,1)S(1)}, bf16[32,2048]{1,0:T(8,128)(2,1)S(1)}, u32[]{:S(2)}, u32[]{:S(2)}) collective-permute-start(bf16[32,2048]{1,0:T(8,128)(2,1)S(1)} %collective-permute-done.19.refs_0_), channel_id=1, source_target_pairs={{0,2},{2,0},{1,3},{3,1},{4,6},{6,4},{5,7},{7,5},{8,10},{10,8},{9,1... | collective-permute-start | bytes 393224 | tf_op jit(solution)/shard_map/ppermute | solution.py:34
  79.8 10.5 %collective-permute-start.31 = (bf16[32,2048]{1,0:T(8,128)(2,1)S(1)}, bf16[32,2048]{1,0:T(8,128)(2,1)S(1)}, u32[]{:S(2)}, u32[]{:S(2)}) collective-permute-start(bf16[32,2048]{1,0:T(8,128)(2,1)S(1)} %get-tuple-element.87), channel_id=1, source_target_pairs={{0,2},{2,0},{1,3},{3,1},{4,6},{6,4},{5,7},{7,5},{8,10},{10,8},{9,1... | collective-permute-start | bytes 393224 | tf_op jit(solution)/shard_map/ppermute | solution.py:34
  86.1 8.5 %collective-permute-start.22 = (bf16[32,2048]{1,0:T(8,128)(2,1)S(1)}, bf16[32,2048]{1,0:T(8,128)(2,1)S(1)}, u32[]{:S(2)}, u32[]{:S(2)}) collective-permute-start(bf16[32,2048]{1,0:T(8,128)(2,1)S(1)} %get-tuple-element.79), channel_id=1, source_target_pairs={{0,2},{2,0},{1,3},{3,1},{4,6},{6,4},{5,7},{7,5},{8,10},{10,8},{9,1... | collective-permute-start | bytes 393224 | tf_op jit(solution)/shard_map/ppermute | solution.py:34
  104.8 10.5 %collective-permute-start.43 = (bf16[32,2048]{1,0:T(8,128)(2,1)S(1)}, bf16[32,2048]{1,0:T(8,128)(2,1)S(1)}, u32[]{:S(2)}, u32[]{:S(2)}) collective-permute-start(bf16[32,2048]{1,0:T(8,128)(2,1)S(1)} %get-tuple-element.94), channel_id=1, source_target_pairs={{0,4},{4,0},{8,12},{12,8},{1,5},{5,1},{9,13},{13,9},{2,6},{6,2},{1... | collective-permute-start | bytes 393224 | tf_op jit(solution)/shard_map/ppermute | solution.py:34
  104.8 12.5 %collective-permute-start.37 = (bf16[32,2048]{1,0:T(8,128)(2,1)S(1)}, bf16[32,2048]{1,0:T(8,128)(2,1)S(1)}, u32[]{:S(2)}, u32[]{:S(2)}) collective-permute-start(bf16[32,2048]{1,0:T(8,128)(2,1)S(1)} %get-tuple-element.89), channel_id=1, source_target_pairs={{0,8},{4,12},{8,0},{12,4},{1,9},{5,13},{9,1},{13,5},{2,10},{6,14},... | collective-permute-start | bytes 393224 | tf_op jit(solution)/shard_map/ppermute | solution.py:34
  116.1 11.9 %collective-permute-start.39 = (bf16[32,2048]{1,0:T(8,128)(2,1)S(1)}, bf16[32,2048]{1,0:T(8,128)(2,1)S(1)}, u32[]{:S(2)}, u32[]{:S(2)}) collective-permute-start(bf16[32,2048]{1,0:T(8,128)(2,1)S(1)} %get-tuple-element.90.refs_2_), channel_id=1, source_target_pairs={{0,2},{2,0},{1,3},{3,1},{4,6},{6,4},{5,7},{7,5},{8,10},{10,8},{9,1... | collective-permute-start | bytes 393224 | tf_op jit(solution)/shard_map/ppermute | solution.py:34
  117.3 10.6 %collective-permute-start.38 = (bf16[32,2048]{1,0:T(8,128)(2,1)S(1)}, bf16[32,2048]{1,0:T(8,128)(2,1)S(1)}, u32[]{:S(2)}, u32[]{:S(2)}) collective-permute-start(bf16[32,2048]{1,0:T(8,128)(2,1)S(1)} %collective-permute-done.37.refs_0_), channel_id=1, source_target_pairs={{0,2},{2,0},{1,3},{3,1},{4,6},{6,4},{5,7},{7,5},{8,10},{10,8},{9,1... | collective-permute-start | bytes 393224 | tf_op jit(solution)/shard_map/ppermute | solution.py:34
  137.1 9.3 %collective-permute-start.48 = (bf16[32,2048]{1,0:T(8,128)(2,1)S(1)}, bf16[32,2048]{1,0:T(8,128)(2,1)S(1)}, u32[]{:S(2)}, u32[]{:S(2)}) collective-permute-start(bf16[32,2048]{1,0:T(8,128)(2,1)S(1)} %shard_map.86), channel_id=1, source_target_pairs={{0,8},{4,12},{8,0},{12,4},{1,9},{5,13},{9,1},{13,5},{2,10},{6,14},... | collective-permute-start | bytes 393224 | tf_op jit(solution)/shard_map/ppermute | solution.py:34
  149.7 10.9 %collective-permute-start.61 = (bf16[32,2048]{1,0:T(8,128)(2,1)S(1)}, bf16[32,2048]{1,0:T(8,128)(2,1)S(1)}, u32[]{:S(2)}, u32[]{:S(2)}) collective-permute-start(bf16[32,2048]{1,0:T(8,128)(2,1)S(1)} %get-tuple-element.107), channel_id=1, source_target_pairs={{0,4},{4,0},{8,12},{12,8},{1,5},{5,1},{9,13},{13,9},{2,6},{6,2},{1... | collective-permute-start | bytes 393224 | tf_op jit(solution)/shard_map/ppermute | solution.py:34
  149.7 12.9 %collective-permute-start.55 = (bf16[32,2048]{1,0:T(8,128)(2,1)S(1)}, bf16[32,2048]{1,0:T(8,128)(2,1)S(1)}, u32[]{:S(2)}, u32[]{:S(2)}) collective-permute-start(bf16[32,2048]{1,0:T(8,128)(2,1)S(1)} %get-tuple-element.102), channel_id=1, source_target_pairs={{0,8},{4,12},{8,0},{12,4},{1,9},{5,13},{9,1},{13,5},{2,10},{6,14},... | collective-permute-start | bytes 393224 | tf_op jit(solution)/shard_map/ppermute | solution.py:34
  161.4 11.8 %collective-permute-start.57 = (bf16[32,2048]{1,0:T(8,128)(2,1)S(1)}, bf16[32,2048]{1,0:T(8,128)(2,1)S(1)}, u32[]{:S(2)}, u32[]{:S(2)}) collective-permute-start(bf16[32,2048]{1,0:T(8,128)(2,1)S(1)} %get-tuple-element.103.refs_2_), channel_id=1, source_target_pairs={{0,2},{2,0},{1,3},{3,1},{4,6},{6,4},{5,7},{7,5},{8,10},{10,8},{9,1... | collective-permute-start | bytes 393224 | tf_op jit(solution)/shard_map/ppermute | solution.py:34
  162.6 10.6 %collective-permute-start.56 = (bf16[32,2048]{1,0:T(8,128)(2,1)S(1)}, bf16[32,2048]{1,0:T(8,128)(2,1)S(1)}, u32[]{:S(2)}, u32[]{:S(2)}) collective-permute-start(bf16[32,2048]{1,0:T(8,128)(2,1)S(1)} %collective-permute-done.55.refs_0_), channel_id=1, source_target_pairs={{0,2},{2,0},{1,3},{3,1},{4,6},{6,4},{5,7},{7,5},{8,10},{10,8},{9,1... | collective-permute-start | bytes 393224 | tf_op jit(solution)/shard_map/ppermute | solution.py:34
  182.4 8.7 %collective-permute-start.66 = (bf16[32,2048]{1,0:T(8,128)(2,1)S(1)}, bf16[32,2048]{1,0:T(8,128)(2,1)S(1)}, u32[]{:S(2)}, u32[]{:S(2)}) collective-permute-start(bf16[32,2048]{1,0:T(8,128)(2,1)S(1)} %shard_map.93), channel_id=1, source_target_pairs={{0,8},{4,12},{8,0},{12,4},{1,9},{5,13},{9,1},{13,5},{2,10},{6,14},... | collective-permute-start | bytes 393224 | tf_op jit(solution)/shard_map/ppermute | solution.py:34
  (55 other events, 313.7 us)
where the time goes:
time: 194 us
  starting transfers between devices  75.8 us (39%)
  waiting for transfers between devices  69.4 us (36%)
  Pallas kernels  42.8 us (22%)
  local copies, waits for them, and re-layouts  5.51 us (3%)
    ppermute x73, starting transfers between devices, swap(): lax.ppermute(value, axis, [(i, i ^ step) for i in range(lax.axis_size(axi...  75.8 us
    ppermute x73, waiting for transfers between devices, swap(): lax.ppermute(value, axis, [(i, i ^ step) for i in range(lax.axis_size(axi...  69.4 us
    pallas_call x32, Pallas kernels, call(): pl.pallas_call(body, out_shape=outs, in_specs=specs, out_specs=[VMEM] * l...  42.8 us
    unnamed x13, local copies, waits for them, and re-layouts  5.48 us
  transfers between devices with their start and end apart: 73, of which 29 were waited for; matrix products, arithmetic and copies ran while one was open for 0% of the time, Pallas kernels for 20%

commit v1 on v0

--- a/solution.py
+++ b/solution.py
@@ -36,14 +36,15 @@
 
 def route_body(tp_count, capacity, relative, place_ref, path_ref, mine_ref, other_ref, pick_ref):
     ep_index, core_index = place_ref[0], place_ref[2]
-    hops, local_rows, _ = path_ref.shape
+    hops, local_rows = path_ref.shape
     slots = mine_ref.shape[2]
     lane = lax.broadcasted_iota(jnp.int32, (local_rows, slots), 1)
     row = lax.broadcasted_iota(jnp.int32, (local_rows, local_rows), 0)
     col = lax.broadcasted_iota(jnp.int32, (local_rows, local_rows), 1)
     earlier = (col < row).astype(BF16)
     for hop in range(hops):
-        expert = path_ref[hop]
+        expert = jnp.broadcast_to(path_ref[hop : hop + 1], (local_rows, local_rows))
+        expert = expert.astype(F32).T.astype(jnp.int32)[:, :1]
         onehot = (expert == lane).astype(F32)
         before = jnp.dot(earlier, onehot.astype(BF16), preferred_element_type=F32)
         rank = jnp.sum(before * onehot, axis=1, keepdims=True).astype(jnp.int32)
@@ -84,24 +85,25 @@
     out_refs = refs[count * sub_count + 4 :]
     width = data[0].shape[1]
     capacity = data[0].shape[0]
+    rows = count * capacity
+    blank = [jnp.zeros((128 - rows, width), BF16)] if rows < 128 else []
     total = 0.0
-    values = []
+    scaled, columns = [], []
     for u in range(sub_count):
-        part = jnp.concatenate([data[i * sub_count + u][...] for i in range(count)], axis=0)
-        part = part.astype(F32)
-        values.append(part)
+        part = [data[i * sub_count + u][...] for i in range(count)] + blank
+        part = jnp.concatenate(part, axis=0).astype(F32)
         total = total + jnp.sum(part * part, axis=-1, keepdims=True)
+        columns.append(pl.ds(pl.multiple_of(lax.bitwise_xor(x, u) * width, width), width))
+        scaled.append((part * gain_ref[:, columns[u]]).astype(BF16))
     scale = lax.rsqrt(total / (width * sub_count) + EPS)
     gate = up = 0.0
     for u in range(sub_count):
-        columns = pl.ds(pl.multiple_of(lax.bitwise_xor(x, u) * width, width), width)
-        normed = (values[u] * scale * gain_ref[:, columns]).astype(BF16)
-        gate = gate + jnp.dot(normed, gate_ref[columns, :], preferred_element_type=F32)
-        up = up + jnp.dot(normed, up_ref[columns, :], preferred_element_type=F32)
+        gate = gate + jnp.dot(scaled[u], gate_ref[columns[u], :], preferred_element_type=F32)
+        up = up + jnp.dot(scaled[u], up_ref[columns[u], :], preferred_element_type=F32)
+    gate, up = gate * scale, up * scale
     hidden = (gate / (1.0 + jnp.exp(-gate)) * up).astype(BF16)
     for u in range(sub_count):
-        columns = pl.ds(pl.multiple_of(lax.bitwise_xor(x, u) * width, width), width)
-        partial = jnp.dot(hidden, down_ref[:, columns], preferred_element_type=F32).astype(BF16)
+        partial = jnp.dot(hidden, down_ref[:, columns[u]], preferred_element_type=F32).astype(BF16)
         for i in range(count):
             out_refs[i * sub_count + u][...] = partial[i * capacity : (i + 1) * capacity]
 
@@ -160,21 +162,28 @@
         return value if s == 0 else swap(value, "ep", s)
 
     far = swap(rows, "tp", 1)
-    square = (hops, local_rows, slots)
-    here, there, pick = call(
-        functools.partial(route_body, tp_count, capacity, relative),
-        [jax.ShapeDtypeStruct(s, BF16) for s in (square, square, (hops, slots, local_rows))],
-        place, path, scalars=1,
-    )
+    path = path.reshape(hops, local_rows)
+
+    def route(first, last):
+        square = (last - first, local_rows, slots)
+        return call(
+            functools.partial(route_body, tp_count, capacity, relative),
+            [jax.ShapeDtypeStruct(s, BF16) for s in (square, square, (last - first, slots, local_rows))],
+            place, path[first:last], scalars=1, flops=1 << 31,
+        )
+
+    routes = [[m[0] for m in route(0, 1)]]
     state, *pieces = call(
         functools.partial(first_body, width),
         [whole] + [piece] * count,
-        place, rows, far, pick[0], scalars=1,
+        place, rows, far, routes[0][2], scalars=1,
     )
     groups = ((2, 0), (3, 1)) if count == 4 else (tuple(range(count)),)
-    order = [s for pair in zip(*groups) for s in pair]
+    order = list(range(count))
     for hop in range(hops):
         if hop == 0:
+            later = route(1, hops)
+            routes += [[m[i] for m in later] for i in range(hops - 1)]
             gate = turn(gate_weight[0])
             up = turn(up_weight[0])
             weights = (gate, up, down_weight[0])
@@ -203,13 +212,13 @@
             state, *pieces = call(
                 functools.partial(home_body, count),
                 [whole] + [piece] * count,
-                *mine, *others, state, here[hop], there[hop], pick[hop + 1],
+                *mine, *others, state, *routes[hop][:2], routes[hop + 1][2],
             )
         else:
             (state,) = call(
                 functools.partial(last_body, count, width),
                 [jax.ShapeDtypeStruct(rows.shape, BF16)],
-                place, *mine, *others, state, here[hop], there[hop], scalars=1,
+                place, *mine, *others, state, *routes[hop][:2], scalars=1,
             )
     return state
 

time: 194 us -> 185 us (0.954)
  Pallas kernels: 42.8 us -> 36.9 us
  local copies, waits for them, and re-layouts: 5.51 us -> 1.49 us
    pallas_call x32 -> x33, Pallas kernels: 42.8 us -> 36.9 us  [call(): pl.pallas_call(body, out_shape=outs, in_specs=specs, out_specs=[VMEM] * l...]
    unnamed x13 -> x16, local copies, waits for them, and re-layouts: 5.48 us -> 0.66 us
  transfers between devices with their start and end apart: 73 -> 73, of which waited for: 29 -> 31; matrix products, arithmetic and copies ran while one was open for 0% -> 0% of each run, Pallas kernels for 20% -> 18%
where the time goes in v1:
time: 185 us
  starting transfers between devices  74.5 us (40%)
  waiting for transfers between devices  71.3 us (39%)
  Pallas kernels  36.9 us (20%)
    ppermute x73, starting transfers between devices, swap(): lax.ppermute(value, axis, [(i, i ^ step) for i in range(lax.axis_size(axi...  74.5 us
    ppermute x73, waiting for transfers between devices, swap(): lax.ppermute(value, axis, [(i, i ^ step) for i in range(lax.axis_size(axi...  71.3 us
    pallas_call x33, Pallas kernels, call(): pl.pallas_call(body, out_shape=outs, in_specs=specs, out_specs=[VMEM] * l...  36.9 us
  transfers between devices with their start and end apart: 73, of which 31 were waited for; matrix products, arithmetic and copies ran while one was open for 0% of the time, Pallas kernels for 18%

profile of v1, /device:TPU:0, one launch (start us, length us, event | category | flops | bytes accessed | tf_op | source)
XLA Modules:
  0.0 184.7 jit_solution(721352859234790003)
XLA Ops:
  3.4 3.6 %collective-permute-start.1 = (bf16[32,2048]{1,0:T(8,128)(2,1)S(1)}, bf16[32,2048]{1,0:T(8,128)(2,1)S(1)}, u32[]{:S(2)}, u32[]{:S(2)}) collective-permute-start(bf16[32,2048]{1,0:T(8,128)(2,1)S(1)} %get-tuple-element.64), channel_id=1, source_target_pairs={{0,8},{4,12},{8,0},{12,4},{1,9},{5,13},{9,1},{13,5},{2,10},{6,14},... | collective-permute-start | bytes 393224 | tf_op jit(solution)/shard_map/ppermute | solution.py:34
  10.1 6.9 %collective-permute-done.1.refs_0_ = bf16[32,2048]{1,0:T(8,128)(2,1)S(1)} collective-permute-done((bf16[32,2048]{1,0:T(8,128)(2,1)S(1)}, bf16[32,2048]{1,0:T(8,128)(2,1)S(1)}, u32[]{:S(2)}, u32[]{:S(2)}) %collective-permute-start.1) | collective-permute-done | bytes 131104 | tf_op jit(solution)/shard_map/ppermute | solution.py:34
  25.0 3.3 %shard_map.68 = (bf16[32,2048]{1,0:T(8,128)(2,1)S(1)}, bf16[32,2048]{1,0:T(8,128)(2,1)S(1)}, bf16[32,2048]{1,0:T(8,128)(2,1)S(1)}, bf16[32,2048]{1,0:T(8,128)(2,1)S(1)}) custom-call(s32[3]{0:T(128)S(1)} %pad_add_fusion.place_ref, bf16[32,2048]{1,0:T(8,128)(2,1)S(1)} %collective-permute-done.1.refs_0_, bf16[32,2048]{1,0:T(8,128)(2,1)S(1)} %collective-permute-done.2.refs_1_, ...), custom_call_target="tpu_custom_call" | custom-call | flops 1107296256 | bytes 18366476 | tf_op jit(solution)/shard_map/pallas_call | solution.py:22
  28.6 3.3 %shard_map.70 = (bf16[32,2048]{1,0:T(8,128)(2,1)S(1)}, bf16[32,2048]{1,0:T(8,128)(2,1)S(1)}, bf16[32,2048]{1,0:T(8,128)(2,1)S(1)}, bf16[32,2048]{1,0:T(8,128)(2,1)S(1)}) custom-call(s32[3]{0:T(128)S(1)} %pad_add_fusion.place_ref, bf16[32,2048]{1,0:T(8,128)(2,1)S(1)} %collective-permute-done.5.refs_0_, bf16[32,2048]{1,0:T(8,128)(2,1)S(1)} %collective-permute-done.6.refs_1_, ...), custom_call_target="tpu_custom_call" | custom-call | flops 1107296256 | bytes 18366476 | tf_op jit(solution)/shard_map/pallas_call | solution.py:22
  35.8 3.5 %collective-permute-start.12 = (bf16[32,2048]{1,0:T(8,128)(2,1)S(1)}, bf16[32,2048]{1,0:T(8,128)(2,1)S(1)}, u32[]{:S(2)}, u32[]{:S(2)}) collective-permute-start(bf16[32,2048]{1,0:T(8,128)(2,1)S(1)} %shard_map.72), channel_id=1, source_target_pairs={{0,8},{4,12},{8,0},{12,4},{1,9},{5,13},{9,1},{13,5},{2,10},{6,14},... | collective-permute-start | bytes 393224 | tf_op jit(solution)/shard_map/ppermute | solution.py:34
  41.2 3.4 %collective-permute-start.14 = (bf16[32,2048]{1,0:T(8,128)(2,1)S(1)}, bf16[32,2048]{1,0:T(8,128)(2,1)S(1)}, u32[]{:S(2)}, u32[]{:S(2)}) collective-permute-start(bf16[32,2048]{1,0:T(8,128)(2,1)S(1)} %shard_map.73), channel_id=1, source_target_pairs={{0,12},{4,8},{8,4},{12,0},{1,13},{5,9},{9,5},{13,1},{2,14},{6,10},... | collective-permute-start | bytes 393224 | tf_op jit(solution)/shard_map/ppermute | solution.py:34
  55.4 3.8 %collective-permute-done.23.refs_0_ = bf16[32,2048]{1,0:T(8,128)(2,1)S(1)} collective-permute-done((bf16[32,2048]{1,0:T(8,128)(2,1)S(1)}, bf16[32,2048]{1,0:T(8,128)(2,1)S(1)}, u32[]{:S(2)}, u32[]{:S(2)}) %collective-permute-start.23) | collective-permute-done | bytes 131104 | tf_op jit(solution)/shard_map/ppermute | solution.py:34
  68.2 3.5 %shard_map.78 = (bf16[32,2048]{1,0:T(8,128)(2,1)S(1)}, bf16[32,2048]{1,0:T(8,128)(2,1)S(1)}, bf16[32,2048]{1,0:T(8,128)(2,1)S(1)}, bf16[32,2048]{1,0:T(8,128)(2,1)S(1)}) custom-call(s32[3]{0:T(128)S(1)} %pad_add_fusion.place_ref, bf16[32,2048]{1,0:T(8,128)(2,1)S(1)} %collective-permute-done.23.refs_0_, bf16[32,2048]{1,0:T(8,128)(2,1)S(1)} %collective-permute-done.24.refs_1_, ...), custom_call_target="tpu_custom_call" | custom-call | flops 1107296256 | bytes 18366476 | tf_op jit(solution)/shard_map/pallas_call | solution.py:22
  73.8 3.3 %shard_map.76 = (bf16[32,2048]{1,0:T(8,128)(2,1)S(1)}, bf16[32,2048]{1,0:T(8,128)(2,1)S(1)}, bf16[32,2048]{1,0:T(8,128)(2,1)S(1)}, bf16[32,2048]{1,0:T(8,128)(2,1)S(1)}) custom-call(s32[3]{0:T(128)S(1)} %pad_add_fusion.place_ref, bf16[32,2048]{1,0:T(8,128)(2,1)S(1)} %collective-permute-done.19.refs_0_, bf16[32,2048]{1,0:T(8,128)(2,1)S(1)} %collective-permute-done.20.refs_1_, ...), custom_call_target="tpu_custom_call" | custom-call | flops 1107296256 | bytes 18366476 | tf_op jit(solution)/shard_map/pallas_call | solution.py:22
  79.2 3.4 %collective-permute-start.28 = (bf16[32,2048]{1,0:T(8,128)(2,1)S(1)}, bf16[32,2048]{1,0:T(8,128)(2,1)S(1)}, u32[]{:S(2)}, u32[]{:S(2)}) collective-permute-start(bf16[32,2048]{1,0:T(8,128)(2,1)S(1)} %shard_map.79), channel_id=1, source_target_pairs={{0,4},{4,0},{8,12},{12,8},{1,5},{5,1},{9,13},{13,9},{2,6},{6,2},{1... | collective-permute-start | bytes 393224 | tf_op jit(solution)/shard_map/ppermute | solution.py:34
  89.7 2.8 %collective-permute-done.30.refs_2_ = bf16[32,2048]{1,0:T(8,128)(2,1)S(1)} collective-permute-done((bf16[32,2048]{1,0:T(8,128)(2,1)S(1)}, bf16[32,2048]{1,0:T(8,128)(2,1)S(1)}, u32[]{:S(2)}, u32[]{:S(2)}) %collective-permute-start.30) | collective-permute-done | bytes 131104 | tf_op jit(solution)/shard_map/ppermute | solution.py:34
  99.0 3.8 %collective-permute-done.41.refs_0_ = bf16[32,2048]{1,0:T(8,128)(2,1)S(1)} collective-permute-done((bf16[32,2048]{1,0:T(8,128)(2,1)S(1)}, bf16[32,2048]{1,0:T(8,128)(2,1)S(1)}, u32[]{:S(2)}, u32[]{:S(2)}) %collective-permute-start.41) | collective-permute-done | bytes 131104 | tf_op jit(solution)/shard_map/ppermute | solution.py:34
  103.7 3.9 %collective-permute-done.43.refs_2_ = bf16[32,2048]{1,0:T(8,128)(2,1)S(1)} collective-permute-done((bf16[32,2048]{1,0:T(8,128)(2,1)S(1)}, bf16[32,2048]{1,0:T(8,128)(2,1)S(1)}, u32[]{:S(2)}, u32[]{:S(2)}) %collective-permute-start.43) | collective-permute-done | bytes 131104 | tf_op jit(solution)/shard_map/ppermute | solution.py:34
  110.4 3.6 %collective-permute-done.44.refs_3_ = bf16[32,2048]{1,0:T(8,128)(2,1)S(1)} collective-permute-done((bf16[32,2048]{1,0:T(8,128)(2,1)S(1)}, bf16[32,2048]{1,0:T(8,128)(2,1)S(1)}, u32[]{:S(2)}, u32[]{:S(2)}) %collective-permute-start.44) | collective-permute-done | bytes 131104 | tf_op jit(solution)/shard_map/ppermute | solution.py:34
  114.0 3.3 %shard_map.85 = (bf16[32,2048]{1,0:T(8,128)(2,1)S(1)}, bf16[32,2048]{1,0:T(8,128)(2,1)S(1)}, bf16[32,2048]{1,0:T(8,128)(2,1)S(1)}, bf16[32,2048]{1,0:T(8,128)(2,1)S(1)}) custom-call(s32[3]{0:T(128)S(1)} %pad_add_fusion.place_ref, bf16[32,2048]{1,0:T(8,128)(2,1)S(1)} %collective-permute-done.41.refs_0_, bf16[32,2048]{1,0:T(8,128)(2,1)S(1)} %collective-permute-done.42.refs_1_, ...), custom_call_target="tpu_custom_call" | custom-call | flops 1107296256 | bytes 18366476 | tf_op jit(solution)/shard_map/pallas_call | solution.py:22
  119.4 3.3 %shard_map.83 = (bf16[32,2048]{1,0:T(8,128)(2,1)S(1)}, bf16[32,2048]{1,0:T(8,128)(2,1)S(1)}, bf16[32,2048]{1,0:T(8,128)(2,1)S(1)}, bf16[32,2048]{1,0:T(8,128)(2,1)S(1)}) custom-call(s32[3]{0:T(128)S(1)} %pad_add_fusion.place_ref, bf16[32,2048]{1,0:T(8,128)(2,1)S(1)} %collective-permute-done.37.refs_0_, bf16[32,2048]{1,0:T(8,128)(2,1)S(1)} %collective-permute-done.38.refs_1_, ...), custom_call_target="tpu_custom_call" | custom-call | flops 1107296256 | bytes 18366476 | tf_op jit(solution)/shard_map/pallas_call | solution.py:22
  133.1 5.0 %collective-permute-done.48.refs_2_ = bf16[32,2048]{1,0:T(8,128)(2,1)S(1)} collective-permute-done((bf16[32,2048]{1,0:T(8,128)(2,1)S(1)}, bf16[32,2048]{1,0:T(8,128)(2,1)S(1)}, u32[]{:S(2)}, u32[]{:S(2)}) %collective-permute-start.48) | collective-permute-done | bytes 131104 | tf_op jit(solution)/shard_map/ppermute | solution.py:34
  141.3 3.2 %collective-permute-start.55 = (bf16[32,2048]{1,0:T(8,128)(2,1)S(1)}, bf16[32,2048]{1,0:T(8,128)(2,1)S(1)}, u32[]{:S(2)}, u32[]{:S(2)}) collective-permute-start(bf16[32,2048]{1,0:T(8,128)(2,1)S(1)} %get-tuple-element.108), channel_id=1, source_target_pairs={{0,8},{4,12},{8,0},{12,4},{1,9},{5,13},{9,1},{13,5},{2,10},{6,14},... | collective-permute-start | bytes 393224 | tf_op jit(solution)/shard_map/ppermute | solution.py:34
  144.5 3.9 %collective-permute-done.59.refs_0_ = bf16[32,2048]{1,0:T(8,128)(2,1)S(1)} collective-permute-done((bf16[32,2048]{1,0:T(8,128)(2,1)S(1)}, bf16[32,2048]{1,0:T(8,128)(2,1)S(1)}, u32[]{:S(2)}, u32[]{:S(2)}) %collective-permute-start.59) | collective-permute-done | bytes 131104 | tf_op jit(solution)/shard_map/ppermute | solution.py:34
  149.0 3.1 %collective-permute-done.61.refs_2_ = bf16[32,2048]{1,0:T(8,128)(2,1)S(1)} collective-permute-done((bf16[32,2048]{1,0:T(8,128)(2,1)S(1)}, bf16[32,2048]{1,0:T(8,128)(2,1)S(1)}, u32[]{:S(2)}, u32[]{:S(2)}) %collective-permute-start.61) | collective-permute-done | bytes 131104 | tf_op jit(solution)/shard_map/ppermute | solution.py:34
  155.0 3.5 %collective-permute-done.62.refs_3_ = bf16[32,2048]{1,0:T(8,128)(2,1)S(1)} collective-permute-done((bf16[32,2048]{1,0:T(8,128)(2,1)S(1)}, bf16[32,2048]{1,0:T(8,128)(2,1)S(1)}, u32[]{:S(2)}, u32[]{:S(2)}) %collective-permute-start.62) | collective-permute-done | bytes 131104 | tf_op jit(solution)/shard_map/ppermute | solution.py:34
  158.5 3.3 %shard_map.92 = (bf16[32,2048]{1,0:T(8,128)(2,1)S(1)}, bf16[32,2048]{1,0:T(8,128)(2,1)S(1)}, bf16[32,2048]{1,0:T(8,128)(2,1)S(1)}, bf16[32,2048]{1,0:T(8,128)(2,1)S(1)}) custom-call(s32[3]{0:T(128)S(1)} %pad_add_fusion.place_ref, bf16[32,2048]{1,0:T(8,128)(2,1)S(1)} %collective-permute-done.59.refs_0_, bf16[32,2048]{1,0:T(8,128)(2,1)S(1)} %collective-permute-done.60.refs_1_, ...), custom_call_target="tpu_custom_call" | custom-call | flops 1107296256 | bytes 18366476 | tf_op jit(solution)/shard_map/pallas_call | solution.py:22
  163.9 3.3 %shard_map.90 = (bf16[32,2048]{1,0:T(8,128)(2,1)S(1)}, bf16[32,2048]{1,0:T(8,128)(2,1)S(1)}, bf16[32,2048]{1,0:T(8,128)(2,1)S(1)}, bf16[32,2048]{1,0:T(8,128)(2,1)S(1)}) custom-call(s32[3]{0:T(128)S(1)} %pad_add_fusion.place_ref, bf16[32,2048]{1,0:T(8,128)(2,1)S(1)} %collective-permute-done.55.refs_0_, bf16[32,2048]{1,0:T(8,128)(2,1)S(1)} %collective-permute-done.56.refs_1_, ...), custom_call_target="tpu_custom_call" | custom-call | flops 1107296256 | bytes 18366476 | tf_op jit(solution)/shard_map/pallas_call | solution.py:22
  177.2 4.6 %collective-permute-done.66.refs_2_ = bf16[32,2048]{1,0:T(8,128)(2,1)S(1)} collective-permute-done((bf16[32,2048]{1,0:T(8,128)(2,1)S(1)}, bf16[32,2048]{1,0:T(8,128)(2,1)S(1)}, u32[]{:S(2)}, u32[]{:S(2)}) %collective-permute-start.66) | collective-permute-done | bytes 131104 | tf_op jit(solution)/shard_map/ppermute | solution.py:34
  (178 shorter events, 95.6 us)
Async XLA Ops:
  3.4 13.7 %collective-permute-start.1 = (bf16[32,2048]{1,0:T(8,128)(2,1)S(1)}, bf16[32,2048]{1,0:T(8,128)(2,1)S(1)}, u32[]{:S(2)}, u32[]{:S(2)}) collective-permute-start(bf16[32,2048]{1,0:T(8,128)(2,1)S(1)} %get-tuple-element.64), channel_id=1, source_target_pairs={{0,8},{4,12},{8,0},{12,4},{1,9},{5,13},{9,1},{13,5},{2,10},{6,14},... | collective-permute-start | bytes 393224 | tf_op jit(solution)/shard_map/ppermute | solution.py:34
  7.0 11.8 %collective-permute-start.5 = (bf16[32,2048]{1,0:T(8,128)(2,1)S(1)}, bf16[32,2048]{1,0:T(8,128)(2,1)S(1)}, u32[]{:S(2)}, u32[]{:S(2)}) collective-permute-start(bf16[32,2048]{1,0:T(8,128)(2,1)S(1)} %get-tuple-element.68), channel_id=1, source_target_pairs={{0,12},{4,8},{8,4},{12,0},{1,13},{5,9},{9,5},{13,1},{2,14},{6,10},... | collective-permute-start | bytes 393224 | tf_op jit(solution)/shard_map/ppermute | solution.py:34
  8.4 10.7 %collective-permute-start.7 = (bf16[32,2048]{1,0:T(8,128)(2,1)S(1)}, bf16[32,2048]{1,0:T(8,128)(2,1)S(1)}, u32[]{:S(2)}, u32[]{:S(2)}) collective-permute-start(bf16[32,2048]{1,0:T(8,128)(2,1)S(1)} %get-tuple-element.69), channel_id=1, source_target_pairs={{0,4},{4,0},{8,12},{12,8},{1,5},{5,1},{9,13},{13,9},{2,6},{6,2},{1... | collective-permute-start | bytes 393224 | tf_op jit(solution)/shard_map/ppermute | solution.py:34
  8.6 16.2 %collective-permute-start.3 = (bf16[32,2048]{1,0:T(8,128)(2,1)S(1)}, bf16[32,2048]{1,0:T(8,128)(2,1)S(1)}, u32[]{:S(2)}, u32[]{:S(2)}) collective-permute-start(bf16[32,2048]{1,0:T(8,128)(2,1)S(1)} %get-tuple-element.65.refs_2_), channel_id=1, source_target_pairs={{0,2},{2,0},{1,3},{3,1},{4,6},{6,4},{5,7},{7,5},{8,10},{10,8},{9,1... | collective-permute-start | bytes 393224 | tf_op jit(solution)/shard_map/ppermute | solution.py:34
  18.8 9.8 %collective-permute-start.6 = (bf16[32,2048]{1,0:T(8,128)(2,1)S(1)}, bf16[32,2048]{1,0:T(8,128)(2,1)S(1)}, u32[]{:S(2)}, u32[]{:S(2)}) collective-permute-start(bf16[32,2048]{1,0:T(8,128)(2,1)S(1)} %collective-permute-done.5.refs_0_), channel_id=1, source_target_pairs={{0,2},{2,0},{1,3},{3,1},{4,6},{6,4},{5,7},{7,5},{8,10},{10,8},{9,1... | collective-permute-start | bytes 393224 | tf_op jit(solution)/shard_map/ppermute | solution.py:34
  19.1 9.6 %collective-permute-start.8 = (bf16[32,2048]{1,0:T(8,128)(2,1)S(1)}, bf16[32,2048]{1,0:T(8,128)(2,1)S(1)}, u32[]{:S(2)}, u32[]{:S(2)}) collective-permute-start(bf16[32,2048]{1,0:T(8,128)(2,1)S(1)} %collective-permute-done.7.refs_2_), channel_id=1, source_target_pairs={{0,2},{2,0},{1,3},{3,1},{4,6},{6,4},{5,7},{7,5},{8,10},{10,8},{9,1... | collective-permute-start | bytes 393224 | tf_op jit(solution)/shard_map/ppermute | solution.py:34
  34.0 11.9 %collective-permute-start.4 = (bf16[32,2048]{1,0:T(8,128)(2,1)S(1)}, bf16[32,2048]{1,0:T(8,128)(2,1)S(1)}, u32[]{:S(2)}, u32[]{:S(2)}) collective-permute-start(bf16[32,2048]{1,0:T(8,128)(2,1)S(1)} %get-tuple-element.67), channel_id=1, source_target_pairs={{0,2},{2,0},{1,3},{3,1},{4,6},{6,4},{5,7},{7,5},{8,10},{10,8},{9,1... | collective-permute-start | bytes 393224 | tf_op jit(solution)/shard_map/ppermute | solution.py:34
  35.8 10.5 %collective-permute-start.12 = (bf16[32,2048]{1,0:T(8,128)(2,1)S(1)}, bf16[32,2048]{1,0:T(8,128)(2,1)S(1)}, u32[]{:S(2)}, u32[]{:S(2)}) collective-permute-start(bf16[32,2048]{1,0:T(8,128)(2,1)S(1)} %shard_map.72), channel_id=1, source_target_pairs={{0,8},{4,12},{8,0},{12,4},{1,9},{5,13},{9,1},{13,5},{2,10},{6,14},... | collective-permute-start | bytes 393224 | tf_op jit(solution)/shard_map/ppermute | solution.py:34
  54.5 11.7 %collective-permute-start.19 = (bf16[32,2048]{1,0:T(8,128)(2,1)S(1)}, bf16[32,2048]{1,0:T(8,128)(2,1)S(1)}, u32[]{:S(2)}, u32[]{:S(2)}) collective-permute-start(bf16[32,2048]{1,0:T(8,128)(2,1)S(1)} %get-tuple-element.80), channel_id=1, source_target_pairs={{0,8},{4,12},{8,0},{12,4},{1,9},{5,13},{9,1},{13,5},{2,10},{6,14},... | collective-permute-start | bytes 393224 | tf_op jit(solution)/shard_map/ppermute | solution.py:34
  63.1 10.7 %collective-permute-start.21 = (bf16[32,2048]{1,0:T(8,128)(2,1)S(1)}, bf16[32,2048]{1,0:T(8,128)(2,1)S(1)}, u32[]{:S(2)}, u32[]{:S(2)}) collective-permute-start(bf16[32,2048]{1,0:T(8,128)(2,1)S(1)} %get-tuple-element.81.refs_2_), channel_id=1, source_target_pairs={{0,2},{2,0},{1,3},{3,1},{4,6},{6,4},{5,7},{7,5},{8,10},{10,8},{9,1... | collective-permute-start | bytes 393224 | tf_op jit(solution)/shard_map/ppermute | solution.py:34
  73.0 9.6 %collective-permute-start.31 = (bf16[32,2048]{1,0:T(8,128)(2,1)S(1)}, bf16[32,2048]{1,0:T(8,128)(2,1)S(1)}, u32[]{:S(2)}, u32[]{:S(2)}) collective-permute-start(bf16[32,2048]{1,0:T(8,128)(2,1)S(1)} %get-tuple-element.91), channel_id=1, source_target_pairs={{0,2},{2,0},{1,3},{3,1},{4,6},{6,4},{5,7},{7,5},{8,10},{10,8},{9,1... | collective-permute-start | bytes 393224 | tf_op jit(solution)/shard_map/ppermute | solution.py:34
  77.1 8.4 %collective-permute-start.29 = (bf16[32,2048]{1,0:T(8,128)(2,1)S(1)}, bf16[32,2048]{1,0:T(8,128)(2,1)S(1)}, u32[]{:S(2)}, u32[]{:S(2)}) collective-permute-start(bf16[32,2048]{1,0:T(8,128)(2,1)S(1)} %get-tuple-element.89), channel_id=1, source_target_pairs={{0,2},{2,0},{1,3},{3,1},{4,6},{6,4},{5,7},{7,5},{8,10},{10,8},{9,1... | collective-permute-start | bytes 393224 | tf_op jit(solution)/shard_map/ppermute | solution.py:34
  78.4 8.5 %collective-permute-start.22 = (bf16[32,2048]{1,0:T(8,128)(2,1)S(1)}, bf16[32,2048]{1,0:T(8,128)(2,1)S(1)}, u32[]{:S(2)}, u32[]{:S(2)}) collective-permute-start(bf16[32,2048]{1,0:T(8,128)(2,1)S(1)} %get-tuple-element.83), channel_id=1, source_target_pairs={{0,2},{2,0},{1,3},{3,1},{4,6},{6,4},{5,7},{7,5},{8,10},{10,8},{9,1... | collective-permute-start | bytes 393224 | tf_op jit(solution)/shard_map/ppermute | solution.py:34
  97.1 10.5 %collective-permute-start.43 = (bf16[32,2048]{1,0:T(8,128)(2,1)S(1)}, bf16[32,2048]{1,0:T(8,128)(2,1)S(1)}, u32[]{:S(2)}, u32[]{:S(2)}) collective-permute-start(bf16[32,2048]{1,0:T(8,128)(2,1)S(1)} %get-tuple-element.100), channel_id=1, source_target_pairs={{0,4},{4,0},{8,12},{12,8},{1,5},{5,1},{9,13},{13,9},{2,6},{6,2},{1... | collective-permute-start | bytes 393224 | tf_op jit(solution)/shard_map/ppermute | solution.py:34
  97.1 12.5 %collective-permute-start.37 = (bf16[32,2048]{1,0:T(8,128)(2,1)S(1)}, bf16[32,2048]{1,0:T(8,128)(2,1)S(1)}, u32[]{:S(2)}, u32[]{:S(2)}) collective-permute-start(bf16[32,2048]{1,0:T(8,128)(2,1)S(1)} %get-tuple-element.95), channel_id=1, source_target_pairs={{0,8},{4,12},{8,0},{12,4},{1,9},{5,13},{9,1},{13,5},{2,10},{6,14},... | collective-permute-start | bytes 393224 | tf_op jit(solution)/shard_map/ppermute | solution.py:34
  108.4 11.0 %collective-permute-start.39 = (bf16[32,2048]{1,0:T(8,128)(2,1)S(1)}, bf16[32,2048]{1,0:T(8,128)(2,1)S(1)}, u32[]{:S(2)}, u32[]{:S(2)}) collective-permute-start(bf16[32,2048]{1,0:T(8,128)(2,1)S(1)} %get-tuple-element.96.refs_2_), channel_id=1, source_target_pairs={{0,2},{2,0},{1,3},{3,1},{4,6},{6,4},{5,7},{7,5},{8,10},{10,8},{9,1... | collective-permute-start | bytes 393224 | tf_op jit(solution)/shard_map/ppermute | solution.py:34
  109.6 9.7 %collective-permute-start.38 = (bf16[32,2048]{1,0:T(8,128)(2,1)S(1)}, bf16[32,2048]{1,0:T(8,128)(2,1)S(1)}, u32[]{:S(2)}, u32[]{:S(2)}) collective-permute-start(bf16[32,2048]{1,0:T(8,128)(2,1)S(1)} %collective-permute-done.37.refs_0_), channel_id=1, source_target_pairs={{0,2},{2,0},{1,3},{3,1},{4,6},{6,4},{5,7},{7,5},{8,10},{10,8},{9,1... | collective-permute-start | bytes 393224 | tf_op jit(solution)/shard_map/ppermute | solution.py:34
  128.5 9.6 %collective-permute-start.48 = (bf16[32,2048]{1,0:T(8,128)(2,1)S(1)}, bf16[32,2048]{1,0:T(8,128)(2,1)S(1)}, u32[]{:S(2)}, u32[]{:S(2)}) collective-permute-start(bf16[32,2048]{1,0:T(8,128)(2,1)S(1)} %shard_map.87), channel_id=1, source_target_pairs={{0,8},{4,12},{8,0},{12,4},{1,9},{5,13},{9,1},{13,5},{2,10},{6,14},... | collective-permute-start | bytes 393224 | tf_op jit(solution)/shard_map/ppermute | solution.py:34
  140.0 8.4 %collective-permute-start.59 = (bf16[32,2048]{1,0:T(8,128)(2,1)S(1)}, bf16[32,2048]{1,0:T(8,128)(2,1)S(1)}, u32[]{:S(2)}, u32[]{:S(2)}) collective-permute-start(bf16[32,2048]{1,0:T(8,128)(2,1)S(1)} %get-tuple-element.112), channel_id=1, source_target_pairs={{0,12},{4,8},{8,4},{12,0},{1,13},{5,9},{9,5},{13,1},{2,14},{6,10},... | collective-permute-start | bytes 393224 | tf_op jit(solution)/shard_map/ppermute | solution.py:34
  141.3 10.9 %collective-permute-start.61 = (bf16[32,2048]{1,0:T(8,128)(2,1)S(1)}, bf16[32,2048]{1,0:T(8,128)(2,1)S(1)}, u32[]{:S(2)}, u32[]{:S(2)}) collective-permute-start(bf16[32,2048]{1,0:T(8,128)(2,1)S(1)} %get-tuple-element.113), channel_id=1, source_target_pairs={{0,4},{4,0},{8,12},{12,8},{1,5},{5,1},{9,13},{13,9},{2,6},{6,2},{1... | collective-permute-start | bytes 393224 | tf_op jit(solution)/shard_map/ppermute | solution.py:34
  141.3 12.9 %collective-permute-start.55 = (bf16[32,2048]{1,0:T(8,128)(2,1)S(1)}, bf16[32,2048]{1,0:T(8,128)(2,1)S(1)}, u32[]{:S(2)}, u32[]{:S(2)}) collective-permute-start(bf16[32,2048]{1,0:T(8,128)(2,1)S(1)} %get-tuple-element.108), channel_id=1, source_target_pairs={{0,8},{4,12},{8,0},{12,4},{1,9},{5,13},{9,1},{13,5},{2,10},{6,14},... | collective-permute-start | bytes 393224 | tf_op jit(solution)/shard_map/ppermute | solution.py:34
  153.0 10.9 %collective-permute-start.57 = (bf16[32,2048]{1,0:T(8,128)(2,1)S(1)}, bf16[32,2048]{1,0:T(8,128)(2,1)S(1)}, u32[]{:S(2)}, u32[]{:S(2)}) collective-permute-start(bf16[32,2048]{1,0:T(8,128)(2,1)S(1)} %get-tuple-element.109.refs_2_), channel_id=1, source_target_pairs={{0,2},{2,0},{1,3},{3,1},{4,6},{6,4},{5,7},{7,5},{8,10},{10,8},{9,1... | collective-permute-start | bytes 393224 | tf_op jit(solution)/shard_map/ppermute | solution.py:34
  154.2 9.7 %collective-permute-start.56 = (bf16[32,2048]{1,0:T(8,128)(2,1)S(1)}, bf16[32,2048]{1,0:T(8,128)(2,1)S(1)}, u32[]{:S(2)}, u32[]{:S(2)}) collective-permute-start(bf16[32,2048]{1,0:T(8,128)(2,1)S(1)} %collective-permute-done.55.refs_0_), channel_id=1, source_target_pairs={{0,2},{2,0},{1,3},{3,1},{4,6},{6,4},{5,7},{7,5},{8,10},{10,8},{9,1... | collective-permute-start | bytes 393224 | tf_op jit(solution)/shard_map/ppermute | solution.py:34
  172.5 9.3 %collective-permute-start.66 = (bf16[32,2048]{1,0:T(8,128)(2,1)S(1)}, bf16[32,2048]{1,0:T(8,128)(2,1)S(1)}, u32[]{:S(2)}, u32[]{:S(2)}) collective-permute-start(bf16[32,2048]{1,0:T(8,128)(2,1)S(1)} %shard_map.94), channel_id=1, source_target_pairs={{0,8},{4,12},{8,0},{12,4},{1,9},{5,13},{9,1},{13,5},{2,10},{6,14},... | collective-permute-start | bytes 393224 | tf_op jit(solution)/shard_map/ppermute | solution.py:34
  (57 other events, 357.1 us)
